TPU v7x, 32 devices: a whole 2x2x4 slice. The times are simulated.
32 devices in a mesh: dp: 4 (over y, core), tensor: 8 (over z, x).
Axes of the slice: x: 2, y: 2, z: 4, core: 2. Of those that a mesh axis runs over, the one named last changes fastest.
Arguments:
- inputs: bfloat16 [8192, 1024], P(('dp', 'tensor')), may hold values from -6 to 6
- qkv_weight: bfloat16 [1024, 3072], P(None, 'tensor'), may hold values from -0.1875 to 0.1875
- qkv_bias: bfloat16 [3072], P('tensor'), may hold values from -3 to 3
- dense_weight: bfloat16 [1024, 1024], P('tensor'), may hold values from -1 to 1
- up_weight: bfloat16 [1024, 4096], P(None, 'tensor'), may hold values from -0.1875 to 0.1875
- up_bias: bfloat16 [4096], P('tensor'), may hold values from -3 to 3
- down_weight: bfloat16 [4096, 1024], P('tensor'), may hold values from -0.09375 to 0.09375
- out_bias: bfloat16 [1024], replicated, may hold values from -3 to 3
- gain_one: bfloat16 [1024], replicated, may hold values from 0.099609375 to 1.8984375
- shift_one: bfloat16 [1024], replicated, may hold values from -2 to 2
- gain_two: bfloat16 [1024], replicated, may hold values from 0.099609375 to 1.8984375
- shift_two: bfloat16 [1024], replicated, may hold values from -2 to 2
- feature_omega: float32 [64, 64], replicated, may hold values from -0.75 to 0.75
- doc_ids: int32 [4, 2048], P('dp'), may hold values from 0 to 7, never falling along the last dimension, each value on 1 to 1024 neighbouring positions
- out_grad: bfloat16 [8192, 1024], P(('dp', 'tensor')), may hold values from -6 to 6
Outputs:
- layer_out: bfloat16 [8192, 1024], P(('dp', 'tensor'))
- input_grad: float32 [8192, 1024], P(('dp', 'tensor'))
- qkv_weight_grad: float32 [1024, 3072], P(None, 'tensor')
- qkv_bias_grad: float32 [3072], P('tensor')
- dense_weight_grad: float32 [1024, 1024], P('tensor')
- up_weight_grad: float32 [1024, 4096], P(None, 'tensor')
- up_bias_grad: float32 [4096], P('tensor')
- down_weight_grad: float32 [4096, 1024], P('tensor')
- out_bias_grad: float32 [1024], P('tensor')
- gain_one_grad: float32 [1024], P('tensor')
- shift_one_grad: float32 [1024], P('tensor')
- gain_two_grad: float32 [1024], P('tensor')
- shift_two_grad: float32 [1024], P('tensor')
Inputs may be any that keep to these rules, and one draw needn't show every extreme that they name: `doc_ids`: in each packed row the document numbers never fall; a document holds at most 1024 tokens and some document holds exactly that many.
All inputs are finite; a program needn't handle non-finite values.
Results may differ from a plain program's by a relative error of at most 0.0072.
Values may be sent and summed in bfloat16 or wider, within the bound.
No kernel may reach another device: no remote copies, remote signals or barrier semaphores. Data moves between devices by JAX's collectives and lax.ppermute only.
A program may use at most 192 MiB of HBM per device.

v0:
```python
import jax
import jax.numpy as jnp
from jax import lax
from jax.sharding import PartitionSpec as P

HEAD_DIM = 64
ROT = 16
LEN = 2048
EPS = 1e-05
EXACT = lax.Precision.HIGHEST


def layer_norm(values, gain_row, offset):
    row_mean = jnp.mean(values, axis=-1, keepdims=True)
    centred = values - row_mean
    spread = jnp.mean(centred * centred, axis=-1, keepdims=True)
    return centred * lax.rsqrt(spread + EPS) * gain_row + offset


def both_norms(token_rows, first_gain, first_offset, second_gain, second_offset):
    return (
        layer_norm(token_rows, first_gain, first_offset),
        layer_norm(token_rows, second_gain, second_offset),
    )


def exact_gelu(values):
    return jax.nn.gelu(values, approximate=False)


def dct_matrix(extent):
    indices = jnp.arange(extent, dtype=jnp.float32)
    cosines = jnp.cos(jnp.pi * (indices[:, None] + 0.5) * indices[None, :] / extent)
    scales = jnp.where(indices == 0, jnp.sqrt(1.0 / extent), jnp.sqrt(2.0 / extent))
    return cosines * scales[None, :]


def rotary_tables(positions, turned):
    half_rot = turned // 2
    frequencies = 10000.0 ** (-(jnp.arange(half_rot, dtype=jnp.float32) * 2.0 / turned))
    angles = positions.astype(jnp.float32)[:, None] * frequencies[None, :]
    return (jnp.cos(angles), jnp.sin(angles))


def rotate(values, cosine_table, sine_table):
    half_rot = cosine_table.shape[-1]
    leading = values[..., :half_rot]
    trailing = values[..., half_rot : 2 * half_rot]
    return jnp.concatenate(
        [
            leading * cosine_table - trailing * sine_table,
            trailing * cosine_table + leading * sine_table,
            values[..., 2 * half_rot :],
        ],
        axis=-1,
    )


def feature_map(values, cosine_table, sine_table, mixing):
    return jnp.exp(jnp.dot(rotate(values, cosine_table, sine_table), mixing, precision=EXACT))


def to_blocks(values, sequences, block_rows):
    shaped = values.reshape(
        (sequences, values.shape[0] // (sequences * block_rows), block_rows) + values.shape[1:]
    )
    return jnp.swapaxes(shaped, 0, 1)


def from_blocks(values):
    joined = jnp.swapaxes(values, 0, 1)
    return joined.reshape((-1,) + joined.shape[3:])


def allowed_pairs(doc_block):
    block_width = doc_block.shape[-1]
    places = jnp.arange(block_width)
    causal = places[:, None] >= places[None, :]
    return (doc_block[:, :, None] == doc_block[:, None, :]) & causal[None]


def attend_forward(query_blocks, key_blocks, value_blocks, doc_blocks, before_docs):
    sequences = query_blocks.shape[1]
    features = query_blocks.shape[-1]
    initial = (
        jnp.zeros((sequences, features, value_blocks.shape[-1]), jnp.float32),
        jnp.zeros((sequences, features), jnp.float32),
    )

    def advance(running, pieces):
        memory, totals = running
        query_rows, key_rows, value_rows, doc_block, before_doc = pieces
        query_wide = query_rows.astype(jnp.float32)
        value_wide = value_rows.astype(jnp.float32)
        weights = jnp.where(
            allowed_pairs(doc_block),
            jnp.einsum("sbf,scf->sbc", query_rows, key_rows, preferred_element_type=jnp.float32),
            0.0,
        )
        carried = (doc_block == before_doc[:, None]).astype(jnp.float32)[:, :, None]
        numerator = jnp.einsum(
            "sbc,sce->sbe", weights, value_wide, precision=EXACT
        ) + carried * jnp.einsum("sbf,sfe->sbe", query_wide, memory, precision=EXACT)
        denominator = (
            jnp.sum(weights, axis=-1, keepdims=True)
            + carried * jnp.einsum("sbf,sf->sb", query_wide, totals, precision=EXACT)[:, :, None]
        )
        last_doc = doc_block[:, -1]
        retained = (last_doc == before_doc).astype(jnp.float32)
        chosen = key_rows * (doc_block == last_doc[:, None]).astype(jnp.bfloat16)[:, :, None]
        new_memory = retained[:, None, None] * memory + jnp.einsum(
            "sbf,sbe->sfe", chosen, value_rows, preferred_element_type=jnp.float32
        )
        new_totals = retained[:, None] * totals + jnp.sum(chosen.astype(jnp.float32), axis=1)
        return ((new_memory, new_totals), (numerator / denominator, denominator, memory, totals))

    final_running, stored = lax.scan(
        advance, initial, (query_blocks, key_blocks, value_blocks, doc_blocks, before_docs)
    )
    return stored


def attend_backward(
    query_blocks,
    key_blocks,
    value_blocks,
    doc_blocks,
    before_docs,
    after_docs,
    stored,
    result_grads,
):
    result_blocks, denominators, memories, totals_before = stored
    sequences = query_blocks.shape[1]
    features = query_blocks.shape[-1]
    initial = (
        jnp.zeros((sequences, features, value_blocks.shape[-1]), jnp.float32),
        jnp.zeros((sequences, features), jnp.float32),
    )

    def retreat(running, pieces):
        later, later_totals = running
        (
            query_rows,
            key_rows,
            value_rows,
            doc_block,
            before_doc,
            after_doc,
            result_rows,
            denominator,
            memory,
            totals,
            result_grad,
        ) = pieces
        query_wide = query_rows.astype(jnp.float32)
        key_wide = key_rows.astype(jnp.float32)
        value_wide = value_rows.astype(jnp.float32)
        allowed = allowed_pairs(doc_block)
        weights = jnp.where(
            allowed,
            jnp.einsum("sbf,scf->sbc", query_rows, key_rows, preferred_element_type=jnp.float32),
            0.0,
        )
        numerator_grad = result_grad / denominator
        denominator_grad = -jnp.sum(result_grad * result_rows, axis=-1, keepdims=True) / denominator
        weight_grad = jnp.where(
            allowed,
            jnp.einsum("sbe,sce->sbc", numerator_grad, value_wide, precision=EXACT)
            + denominator_grad,
            0.0,
        )
        carried = (doc_block == before_doc[:, None]).astype(jnp.float32)[:, :, None]
        query_grad = jnp.einsum(
            "sbc,scf->sbf", weight_grad, key_wide, precision=EXACT
        ) + carried * (
            jnp.einsum("sbe,sfe->sbf", numerator_grad, memory, precision=EXACT)
            + denominator_grad * totals[:, None, :]
        )
        linked = (doc_block == after_doc[:, None]).astype(jnp.float32)[:, :, None]
        key_grad = jnp.einsum("sbc,sbf->scf", weight_grad, query_wide, precision=EXACT) + linked * (
            jnp.einsum("sbe,sfe->sbf", value_wide, later, precision=EXACT)
            + later_totals[:, None, :]
        )
        value_grad = jnp.einsum(
            "sbc,sbe->sce", weights, numerator_grad, precision=EXACT
        ) + linked * jnp.einsum("sbf,sfe->sbe", key_wide, later, precision=EXACT)
        first_doc = doc_block[:, 0]
        retained = (first_doc == after_doc).astype(jnp.float32)
        chosen = query_wide * (doc_block == first_doc[:, None]).astype(jnp.float32)[:, :, None]
        new_later = retained[:, None, None] * later + jnp.einsum(
            "sbf,sbe->sfe", chosen, numerator_grad, precision=EXACT
        )
        new_totals = retained[:, None] * later_totals + jnp.sum(chosen * denominator_grad, axis=1)
        return ((new_later, new_totals), (query_grad, key_grad, value_grad))

    final_running, grads = lax.scan(
        retreat,
        initial,
        (
            query_blocks,
            key_blocks,
            value_blocks,
            doc_blocks,
            before_docs,
            after_docs,
            result_blocks,
            denominators,
            memories,
            totals_before,
            result_grads,
        ),
        reverse=True,
    )
    return grads


def on_device(
    inputs,
    qkv_weight,
    qkv_bias,
    dense_weight,
    up_weight,
    up_bias,
    down_weight,
    out_bias,
    gain_one,
    shift_one,
    gain_two,
    shift_two,
    feature_omega,
    doc_ids,
    out_grad,
):
    local_rows = inputs.astype(jnp.float32)
    model_width = local_rows.shape[1]
    first_gain = gain_one.astype(jnp.float32)
    second_gain = gain_two.astype(jnp.float32)
    norm_values, norm_pull = jax.vjp(
        both_norms,
        local_rows,
        first_gain,
        shift_one.astype(jnp.float32),
        second_gain,
        shift_two.astype(jnp.float32),
    )
    whole_one, whole_two = (
        lax.all_gather(norm_values[0].astype(jnp.bfloat16), "tensor", axis=0, tiled=True),
        lax.all_gather(norm_values[1].astype(jnp.bfloat16), "tensor", axis=0, tiled=True),
    )
    group_rows = whole_one.shape[0]
    sequences = doc_ids.shape[0]
    block_rows = min(512, LEN // 4)
    projected = jnp.dot(
        whole_one, qkv_weight, preferred_element_type=jnp.float32
    ) + qkv_bias.astype(jnp.float32)
    hidden = jnp.dot(whole_two, up_weight, preferred_element_type=jnp.float32) + up_bias.astype(
        jnp.float32
    )
    activated_exact, gelu_pull = jax.vjp(exact_gelu, hidden)
    activated = activated_exact.astype(jnp.bfloat16)
    cosine_table, sine_table = rotary_tables(jnp.arange(group_rows) % LEN, ROT)
    mixing = jnp.dot(dct_matrix(HEAD_DIM), feature_omega, precision=EXACT)
    doc_blocks = to_blocks(doc_ids.reshape(group_rows), sequences, block_rows)
    before_docs = jnp.concatenate(
        [jnp.full((1, sequences), -1, jnp.int32), doc_blocks[:-1, :, -1]], axis=0
    )
    after_docs = jnp.concatenate(
        [doc_blocks[1:, :, 0], jnp.full((1, sequences), -1, jnp.int32)], axis=0
    )

    def features_of(token_rows):
        return feature_map(token_rows, cosine_table, sine_table, mixing)

    local_heads = qkv_weight.shape[1] // (3 * HEAD_DIM)
    head_saved = []
    head_results = []
    for head_index in range(local_heads):
        column_base = head_index * 3 * HEAD_DIM
        query_exact, query_pull = jax.vjp(
            features_of, projected[:, column_base : column_base + HEAD_DIM]
        )
        key_exact, key_pull = jax.vjp(
            features_of, projected[:, column_base + HEAD_DIM : column_base + 2 * HEAD_DIM]
        )
        value_rows = projected[:, column_base + 2 * HEAD_DIM : column_base + 3 * HEAD_DIM].astype(
            jnp.bfloat16
        )
        blocks = (
            to_blocks(query_exact.astype(jnp.bfloat16), sequences, block_rows),
            to_blocks(key_exact.astype(jnp.bfloat16), sequences, block_rows),
            to_blocks(value_rows, sequences, block_rows),
        )
        stored = attend_forward(blocks[0], blocks[1], blocks[2], doc_blocks, before_docs)
        head_results.append(from_blocks(stored[0]))
        head_saved.append((blocks, stored, query_pull, key_pull))
    merged = jnp.concatenate(head_results, axis=1).astype(jnp.bfloat16)
    branch_total = lax.psum_scatter(
        jnp.dot(merged, dense_weight, preferred_element_type=jnp.float32),
        "tensor",
        scatter_dimension=0,
        tiled=True,
    ) + lax.psum_scatter(
        jnp.dot(activated, down_weight, preferred_element_type=jnp.float32).astype(jnp.bfloat16),
        "tensor",
        scatter_dimension=0,
        tiled=True,
    ).astype(
        jnp.float32
    )
    layer_out = (local_rows + branch_total + out_bias.astype(jnp.float32)).astype(jnp.bfloat16)
    grad_whole = lax.all_gather(out_grad, "tensor", axis=0, tiled=True)
    merged_grad = jnp.einsum(
        "td,ed->te", grad_whole, dense_weight, preferred_element_type=jnp.float32
    )
    dense_weight_grad = jnp.einsum(
        "te,td->ed", merged, grad_whole, preferred_element_type=jnp.float32
    )
    down_weight_grad = jnp.einsum(
        "tf,td->fd", activated, grad_whole, preferred_element_type=jnp.float32
    )
    activated_grad = jnp.einsum(
        "td,fd->tf", grad_whole, down_weight, preferred_element_type=jnp.float32
    )
    hidden_grad = gelu_pull(activated_grad)[0].astype(jnp.bfloat16)
    up_weight_grad = jnp.einsum(
        "td,tf->df", whole_two, hidden_grad, preferred_element_type=jnp.float32
    )
    up_bias_grad = jnp.sum(hidden_grad, axis=0, dtype=jnp.float32)
    column_grads = []
    for head_index in range(local_heads):
        blocks, stored, query_pull, key_pull = head_saved[head_index]
        result_grads = to_blocks(
            merged_grad[:, head_index * HEAD_DIM : (head_index + 1) * HEAD_DIM],
            sequences,
            block_rows,
        )
        query_grad, key_grad, value_grad = attend_backward(
            blocks[0],
            blocks[1],
            blocks[2],
            doc_blocks,
            before_docs,
            after_docs,
            stored,
            result_grads,
        )
        column_grads.extend(
            [
                query_pull(from_blocks(query_grad))[0],
                key_pull(from_blocks(key_grad))[0],
                from_blocks(value_grad),
            ]
        )
    qkv_grad = jnp.concatenate(column_grads, axis=1).astype(jnp.bfloat16)
    qkv_weight_grad = jnp.einsum(
        "td,tc->dc", whole_one, qkv_grad, preferred_element_type=jnp.float32
    )
    qkv_bias_grad = jnp.sum(qkv_grad, axis=0, dtype=jnp.float32)
    local_grad = out_grad.astype(jnp.float32)
    norm_grads = lax.psum_scatter(
        jnp.concatenate(
            [
                jnp.einsum("tc,dc->td", qkv_grad, qkv_weight, preferred_element_type=jnp.float32),
                jnp.einsum("tf,df->td", hidden_grad, up_weight, preferred_element_type=jnp.float32),
            ],
            axis=1,
        ),
        "tensor",
        scatter_dimension=0,
        tiled=True,
    )
    row_part, first_gain_grad, first_shift_grad, second_gain_grad, second_shift_grad = norm_pull(
        (norm_grads[:, :model_width], norm_grads[:, model_width:])
    )
    input_grad = local_grad + row_part
    vector_part = lax.psum_scatter(
        jnp.stack(
            [
                first_gain_grad,
                first_shift_grad,
                second_gain_grad,
                second_shift_grad,
                jnp.sum(local_grad, axis=0),
            ]
        ),
        "tensor",
        scatter_dimension=1,
        tiled=True,
    )
    summed = lax.psum(
        (
            qkv_weight_grad,
            qkv_bias_grad,
            dense_weight_grad,
            up_weight_grad,
            up_bias_grad,
            down_weight_grad,
            vector_part,
        ),
        "dp",
    )
    vectors = summed[6]
    return (
        layer_out,
        input_grad,
        summed[0],
        summed[1],
        summed[2],
        summed[3],
        summed[4],
        summed[5],
        vectors[4],
        vectors[0],
        vectors[1],
        vectors[2],
        vectors[3],
    )


def solution(mesh):
    in_specs = (
        P(("dp", "tensor"), None),
        P(None, "tensor"),
        P("tensor"),
        P("tensor", None),
        P(None, "tensor"),
        P("tensor"),
        P("tensor", None),
        P(),
        P(),
        P(),
        P(),
        P(),
        P(),
        P("dp", None),
        P(("dp", "tensor"), None),
    )
    out_specs = (
        P(("dp", "tensor"), None),
        P(("dp", "tensor"), None),
        P(None, "tensor"),
        P("tensor"),
        P("tensor", None),
        P(None, "tensor"),
        P("tensor"),
        P("tensor", None),
        P("tensor"),
        P("tensor"),
        P("tensor"),
        P("tensor"),
        P("tensor"),
    )
    return jax.shard_map(
        on_device, mesh=mesh, in_specs=in_specs, out_specs=out_specs, check_vma=False
    )
```

profile of v0, /device:TPU:0, one launch (start us, length us, event | category | flops | bytes accessed | tf_op | source)
XLA Modules:
  0.0 1256.8 jit_solution(18088975919537195365)
XLA Ops:
  22.2 64.1 %all-gather.8.cloned.1.call-done = bf16[2048,1024]{1,0:T(8,128)(2,1)} async-done(((bf16[256,1024]{1,0:T(8,128)(2,1)}), bf16[2048,1024]{1,0:T(8,128)(2,1)}) %all-gather.8.cloned.1.call-update) | async-done | bytes 4194320 | tf_op jit(solution)/shard_map/all_gather | solution.py:312
  86.4 3.7 fusion.330
  91.8 68.9 %all-gather.4.cloned.1.call-done = bf16[2048,1024]{1,0:T(8,128)(2,1)} async-done(((bf16[256,1024]{1,0:T(8,128)(2,1)}), bf16[2048,1024]{1,0:T(8,128)(2,1)}) %all-gather.4.cloned.1.call-update) | async-done | bytes 4194320 | tf_op jit(solution)/shard_map/all_gather | solution.py:248
  160.7 5.7 fusion.325
  179.6 37.3 %while.89 = (s32[]{:T(128)}, f32[1,64,64]{2,1,0:T(8,128)S(1)}, f32[1,64]{1,0:T(1,128)S(1)}, f32[4,1,512,64]{2,3,1,0:T(8,128)}, f32[4,1,512,1]{2,3,1,0:T(1,128)},...) while((s32[]{:T(128)}, f32[1,64,64]{2,1,0:T(8,128)S(1)}, ...), condition=%wide.region_9.10_spmd.clone, body=%wide.region_6.9_spmd.clone.sunk | while | flops 266197760 | bytes 3668453 | solution.py:117
  218.7 125.6 %while.91 = (s32[]{:T(128)}, f32[1,64,64]{2,1,0:T(8,128)}, f32[1,64]{1,0:T(1,128)}, f32[4,1,512,64]{2,0,3,1:T(4,128)}, f32[4,1,512,64]{2,0,3,1:T(4,128)}, /*inde...) while((s32[]{:T(128)}, f32[1,64,64]{2,1,0:T(8,128)}, ...), condition=%wide.region_19.20_spmd.clone, body=%wide.region_16.19_spmd.clone.sunk | while | flops 942595712 | bytes 11318790 | solution.py:197
  236.9 3.6 dynamic_update_slice.133
  240.6 3.6 dynamic_update_slice.132
  268.5 3.6 dynamic_update_slice.133
  272.2 3.6 dynamic_update_slice.132
  300.1 3.6 dynamic_update_slice.133
  303.7 3.6 dynamic_update_slice.132
  331.6 3.6 dynamic_update_slice.133
  335.3 3.6 dynamic_update_slice.132
  350.8 35.3 %while.88 = (s32[]{:T(128)}, f32[1,64,64]{2,1,0:T(8,128)S(1)}, f32[1,64]{1,0:T(1,128)S(1)}, f32[4,1,512,64]{2,3,1,0:T(8,128)}, f32[4,1,512,1]{2,3,1,0:T(1,128)S(...) while((s32[]{:T(128)}, f32[1,64,64]{2,1,0:T(8,128)S(1)}, ...), condition=%wide.region_5.6_spmd.clone, body=%wide.region_2.5_spmd.clone.sunk | while | flops 266197760 | bytes 3668709 | solution.py:117
  387.8 107.8 %while.90 = (s32[]{:T(128)}, f32[1,64,64]{2,1,0:T(8,128)}, f32[1,64]{1,0:T(1,128)}, f32[4,1,512,64]{2,0,3,1:T(4,128)}, f32[4,1,512,64]{2,0,3,1:T(4,128)}, /*inde...) while((s32[]{:T(128)}, f32[1,64,64]{2,1,0:T(8,128)}, ...), condition=%wide.region_15.16_spmd.clone, body=%wide.region_12.15_spmd.clone.sunk | while | flops 942595712 | bytes 11392122 | solution.py:197
  392.9 2.5 compare_convert_fusion.14
  403.7 3.6 dynamic_update_slice.130
  407.3 3.6 dynamic_update_slice.129
  419.3 2.5 compare_convert_fusion.14
  430.7 3.6 dynamic_update_slice.130
  434.4 3.6 dynamic_update_slice.129
  446.4 2.5 compare_convert_fusion.14
  457.8 3.6 dynamic_update_slice.130
  461.4 3.6 dynamic_update_slice.129
  473.5 2.5 compare_convert_fusion.14
  484.8 3.6 dynamic_update_slice.130
  488.5 3.6 dynamic_update_slice.129
  504.6 5.7 fusion.331
  510.3 5.0 fusion.329
  515.4 13.6 %convert_reduce_fusion.2 = (f32[512]{0:T(512)S(1)}, bf16[2048,512]{1,0:T(8,128)(2,1)S(1)}, f32[2048,512]{1,0:T(8,128)}) fusion(f32[2048,512]{1,0:T(8,128)S(1)} %fusion.329, f32[512]{0:T(512)S(1)} %copy-done.62, bf16[2048,1024]{1,0:T(8,128)(2,1)S(1)} %copy-done.1, bf16[512,1024]{1,0:T(8,128)(2,1)S(1)} %copy-done), kind=kOutput, calls=%fused_computation.269 | convolution fusion | flops 2226126336 | bytes 15732736 | tf_op jit(solution)/shard_map/td,fd->tf/dot_general | solution.py:322
  532.7 6.3 pad_maximum_fusion
  539.1 4.6 multiply_convert_fusion
  545.0 4.3 convolution_convert_fusion
  552.9 4.6 fusion.328
  558.2 5.9 fusion.333
  564.0 3.7 fusion.335
  567.7 3.7 fusion.336
  571.4 248.1 %reduce-scatter.9.cloned.1.call-done = f32[256,2048]{1,0:T(8,128)} async-done(((f32[2048,2048]{1,0:T(8,128)}), f32[256,2048]{1,0:T(8,128)}) %reduce-scatter.9.cloned.1.call-update) | async-done | bytes 2097168 | tf_op jit(solution)/shard_map/reduce_scatter | solution.py:361
  821.9 2.6 fusion.205
  824.5 85.9 %reduce-scatter.7.cloned.1.call-done = bf16[256,1024]{1,0:T(8,128)(2,1)} async-done(((bf16[2048,1024]{1,0:T(8,128)(2,1)}), bf16[256,1024]{1,0:T(8,128)(2,1)}) %reduce-scatter.7.cloned.1.call-update) | async-done | bytes 524304 | tf_op jit(solution)/shard_map/reduce_scatter | solution.py:303
  910.4 152.3 %reduce-scatter.5.cloned.1.call-done = f32[256,1024]{1,0:T(8,128)} async-done(((f32[2048,1024]{1,0:T(8,128)}), f32[256,1024]{1,0:T(8,128)}) %reduce-scatter.5.cloned.1.call-update) | async-done | bytes 1048592 | tf_op jit(solution)/shard_map/reduce_scatter | solution.py:298
  1062.7 3.5 convert_reduce_fusion.5
  1067.0 3.9 fusion.334
  1072.5 47.0 %reduce-scatter.11.cloned.1.call-done = f32[5,128]{1,0:T(8,128)} async-done(((f32[5,1024]{1,0:T(8,128)}), f32[5,128]{1,0:T(8,128)}) %reduce-scatter.11.cloned.1.call-update) | async-done | bytes 2576 | tf_op jit(solution)/shard_map/reduce_scatter | solution.py:377
  1119.6 6.4 all-reduce.12
  1126.5 115.6 %all-reduce.16.cloned.1.call-done = (f32[1024,384]{1,0:T(8,128)}, f32[128,1024]{1,0:T(8,128)}, f32[1024,512]{1,0:T(8,128)}, f32[512,1024]{1,0:T(8,128)}) async-done(((f32[1024,384]{1,0:T(8,128)}, f32[128,1024]{1,0:T(8,128)}, f32[1024,512]{1,0:T(8,128)}, f32[512,1024]{1,0:T(8,128)}), (f32[1024,384]{1,0:T(8,128)}, f32[128,1024]{1,0:T(8,128)}, f32[1024,512]{1,0:T(8,128)}, ...) | async-done | bytes 6291472 | tf_op jit(solution)/shard_map/psum | solution.py:391
  1242.2 2.8 copy.249
  (705 shorter events, 292.0 us)
Async XLA Ops:
  7.2 508.1 %copy-start = (bf16[512,1024]{1,0:T(8,128)(2,1)S(1)}, bf16[512,1024]{1,0:T(8,128)(2,1)}, u32[]{:S(2)}) copy-start(bf16[512,1024]{1,0:T(8,128)(2,1)} %param.29) | copy-start | bytes 3145732
  7.2 14.1 %copy-start.68 = (bf16[512]{0:T(512)(128)(2,1)S(1)}, bf16[512]{0:T(512)(128)(2,1)}, u32[]{:S(2)}) copy-start(bf16[512]{0:T(512)(128)(2,1)} %param.28) | copy-start | bytes 3076
  7.2 14.6 %copy-start.69 = (bf16[384]{0:T(512)(128)(2,1)S(1)}, bf16[384]{0:T(512)(128)(2,1)}, u32[]{:S(2)}) copy-start(bf16[384]{0:T(512)(128)(2,1)} %param.25) | copy-start | bytes 2308
  7.2 14.6 %copy-start.56 = (f32[64,64]{1,0:T(8,128)S(1)}, f32[64,64]{1,0:T(8,128)}, u32[]{:S(2)}) copy-start(f32[64,64]{1,0:T(8,128)} %param.35) | copy-start | bytes 49156
  7.2 79.1 %copy-start.30 = (bf16[128,1024]{1,0:T(8,128)(2,1)S(1)}, bf16[128,1024]{1,0:T(8,128)(2,1)}, u32[]{:S(2)}) copy-start(bf16[128,1024]{1,0:T(8,128)(2,1)} %param.26) | copy-start | bytes 786436
  7.2 79.1 %all-gather.8.cloned.1.call-start = ((), (), s32[]{:S(2)}) async-start(), calls=%async_computation.8 | async-start | bytes 4718592 | tf_op jit(solution)/shard_map/all_gather | solution.py:312
  8.0 152.7 %all-gather.4.cloned.1.call-start = ((), (), s32[]{:S(2)}) async-start(), calls=%async_computation.4 | async-start | bytes 4718592 | tf_op jit(solution)/shard_map/all_gather | solution.py:248
  8.7 77.6 %copy-start.46 = (f32[1024]{0:T(1024)}, f32[1024]{0:T(1024)S(1)}, u32[]{:S(2)}) copy-start(f32[1024]{0:T(1024)S(1)} %convert_element_type.410) | copy-start | bytes 12292
  9.4 76.9 %copy-start.48 = (f32[1024]{0:T(1024)}, f32[1024]{0:T(1024)S(1)}, u32[]{:S(2)}) copy-start(f32[1024]{0:T(1024)S(1)} %convert_element_type.419) | copy-start | bytes 12292
  12.0 74.4 %copy-start.54 = (f32[256]{0:T(256)}, f32[256]{0:T(256)S(1)}, u32[]{:S(2)}) copy-start(f32[256]{0:T(256)S(1)} %broadcast_multiply_fusion) | copy-start | bytes 3076
  13.3 73.0 %copy-start.60 = (f32[256]{0:T(256)}, f32[256]{0:T(256)S(1)}, u32[]{:S(2)}) copy-start(f32[256]{0:T(256)S(1)} %fusion.206) | copy-start | bytes 3076
  13.3 73.0 %copy-start.58 = (f32[256]{0:T(256)}, f32[256]{0:T(256)S(1)}, u32[]{:S(2)}) copy-start(f32[256]{0:T(256)S(1)} %fusion.304) | copy-start | bytes 3076
  15.7 494.6 %all-gather.6.cloned.1.call-start = ((), (), s32[]{:S(2)}) async-start(), calls=%async_computation.6 | async-start | bytes 4718592 | tf_op jit(solution)/shard_map/all_gather | solution.py:249
  16.5 803.1 %reduce-scatter.9.cloned.1.call-start = ((), (), s32[]{:S(2)}) async-start(), calls=%async_computation.9 | async-start | bytes 18874368 | tf_op jit(solution)/shard_map/reduce_scatter | solution.py:361
  22.2 152.6 %copy-start.15 = (f32[64,64]{1,0:T(8,128)}, f32[64,64]{1,0:T(8,128)S(1)}, u32[]{:S(2)}) copy-start(f32[64,64]{1,0:T(8,128)S(1)} %fusion.291) | copy-start | bytes 49156
  90.1 70.7 %copy-start.33 = (bf16[1024,384]{1,0:T(8,128)(2,1)S(1)}, bf16[1024,384]{1,0:T(8,128)(2,1)}, u32[]{:S(2)}) copy-start(bf16[1024,384]{1,0:T(8,128)(2,1)} %param.24) | copy-start | bytes 2359300
  228.5 15.7 %copy-start.38 = (s32[1,1,512]{2,1,0:T(1,128)S(1)}, s32[1,1,512]{2,1,0:T(1,128)}, u32[]{:S(2)}) copy-start(s32[1,1,512]{2,1,0:T(1,128)} %copy-done.37) | copy-start | bytes 6148 | tf_op jit(solution)/shard_map/while
  233.7 12.6 %copy-start.13 = (f32[1,64,64]{2,1,0:T(8,128)S(1)}, f32[1,64,64]{2,1,0:T(8,128)}, u32[]{:S(2)}) copy-start(f32[1,64,64]{2,1,0:T(8,128)} %get-tuple-element.1812) | copy-start | bytes 49156 | tf_op jit(solution)/shard_map/while
  259.4 16.4 %copy-start.38 = (s32[1,1,512]{2,1,0:T(1,128)S(1)}, s32[1,1,512]{2,1,0:T(1,128)}, u32[]{:S(2)}) copy-start(s32[1,1,512]{2,1,0:T(1,128)} %copy-done.37) | copy-start | bytes 6148 | tf_op jit(solution)/shard_map/while
  265.3 12.6 %copy-start.13 = (f32[1,64,64]{2,1,0:T(8,128)S(1)}, f32[1,64,64]{2,1,0:T(8,128)}, u32[]{:S(2)}) copy-start(f32[1,64,64]{2,1,0:T(8,128)} %get-tuple-element.1812) | copy-start | bytes 49156 | tf_op jit(solution)/shard_map/while
  291.0 16.4 %copy-start.38 = (s32[1,1,512]{2,1,0:T(1,128)S(1)}, s32[1,1,512]{2,1,0:T(1,128)}, u32[]{:S(2)}) copy-start(s32[1,1,512]{2,1,0:T(1,128)} %copy-done.37) | copy-start | bytes 6148 | tf_op jit(solution)/shard_map/while
  296.8 12.6 %copy-start.13 = (f32[1,64,64]{2,1,0:T(8,128)S(1)}, f32[1,64,64]{2,1,0:T(8,128)}, u32[]{:S(2)}) copy-start(f32[1,64,64]{2,1,0:T(8,128)} %get-tuple-element.1812) | copy-start | bytes 49156 | tf_op jit(solution)/shard_map/while
  322.6 16.4 %copy-start.38 = (s32[1,1,512]{2,1,0:T(1,128)S(1)}, s32[1,1,512]{2,1,0:T(1,128)}, u32[]{:S(2)}) copy-start(s32[1,1,512]{2,1,0:T(1,128)} %copy-done.37) | copy-start | bytes 6148 | tf_op jit(solution)/shard_map/while
  328.4 12.6 %copy-start.13 = (f32[1,64,64]{2,1,0:T(8,128)S(1)}, f32[1,64,64]{2,1,0:T(8,128)}, u32[]{:S(2)}) copy-start(f32[1,64,64]{2,1,0:T(8,128)} %get-tuple-element.1812) | copy-start | bytes 49156 | tf_op jit(solution)/shard_map/while
  396.5 14.5 %copy-start.40 = (s32[1,1,512]{2,1,0:T(1,128)S(1)}, s32[1,1,512]{2,1,0:T(1,128)}, u32[]{:S(2)}) copy-start(s32[1,1,512]{2,1,0:T(1,128)} %copy-done.39) | copy-start | bytes 6148 | tf_op jit(solution)/shard_map/while
  423.0 15.0 %copy-start.40 = (s32[1,1,512]{2,1,0:T(1,128)S(1)}, s32[1,1,512]{2,1,0:T(1,128)}, u32[]{:S(2)}) copy-start(s32[1,1,512]{2,1,0:T(1,128)} %copy-done.39) | copy-start | bytes 6148 | tf_op jit(solution)/shard_map/while
  429.2 12.2 copy-start.53
  450.0 15.1 %copy-start.40 = (s32[1,1,512]{2,1,0:T(1,128)S(1)}, s32[1,1,512]{2,1,0:T(1,128)}, u32[]{:S(2)}) copy-start(s32[1,1,512]{2,1,0:T(1,128)} %copy-done.39) | copy-start | bytes 6148 | tf_op jit(solution)/shard_map/while
  456.3 12.3 copy-start.53
  456.3 12.2 copy-start.67
  477.1 15.1 %copy-start.40 = (s32[1,1,512]{2,1,0:T(1,128)S(1)}, s32[1,1,512]{2,1,0:T(1,128)}, u32[]{:S(2)}) copy-start(s32[1,1,512]{2,1,0:T(1,128)} %copy-done.39) | copy-start | bytes 6148 | tf_op jit(solution)/shard_map/while
  483.3 12.3 copy-start.53
  483.4 12.2 copy-start.67
  504.6 53.6 %copy-start.4 = (bf16[2048,384]{0,1:T(8,128)(2,1)}, bf16[2048,384]{0,1:T(8,128)(2,1)S(1)}, u32[]{:S(2)}) copy-start(bf16[2048,384]{0,1:T(8,128)(2,1)S(1)} %constant_dynamic-update-slice_fusion.6) | copy-start | bytes 4718596
  510.3 22.4 %slice-start = ((s8[8388608]{0:T(1024)(128)(4,1)}), s8[4194304]{0:T(1024)(128)(4,1)S(1)}, s32[]{:S(2)}) async-start(s8[8388608]{0:T(1024)(128)(4,1)} %bitcast.597), calls=%async_computation.12 | async-start | bytes 8388608
  515.3 13.6 %copy-start.9 = (f32[2048,512]{1,0:T(8,128)}, f32[2048,512]{1,0:T(8,128)S(1)}, u32[]{:S(2)}) copy-start(f32[2048,512]{1,0:T(8,128)S(1)} %fusion.329) | copy-start | bytes 12582916
  515.4 14.9 %copy-start.70 = (bf16[1024,512]{1,0:T(8,128)(2,1)S(1)}, bf16[1024,512]{1,0:T(8,128)(2,1)}, u32[]{:S(2)}) copy-start(bf16[1024,512]{1,0:T(8,128)(2,1)} %param.27) | copy-start | bytes 3145732
  515.4 17.3 %slice-start.1 = ((s8[8388608]{0:T(1024)(128)(4,1)}), s8[4194304]{0:T(1024)(128)(4,1)S(1)}, s32[]{:S(2)}) async-start(s8[8388608]{0:T(1024)(128)(4,1)} %bitcast.597), calls=%async_computation.13 | async-start | bytes 8388608
  539.0 371.4 %reduce-scatter.7.cloned.1.call-start = ((), (), s32[]{:S(2)}) async-start(), calls=%async_computation.7 | async-start | bytes 4718592 | tf_op jit(solution)/shard_map/reduce_scatter | solution.py:303
  549.4 513.4 %reduce-scatter.5.cloned.1.call-start = ((), (), s32[]{:S(2)}) async-start(), calls=%async_computation.5 | async-start | bytes 9437184 | tf_op jit(solution)/shard_map/reduce_scatter | solution.py:298
  557.5 562.1 %reduce-scatter.11.cloned.1.call-start = ((), (), s32[]{:S(2)}) async-start(), calls=%async_computation.10 | async-start | bytes 36864 | tf_op jit(solution)/shard_map/reduce_scatter | solution.py:377
  567.7 251.8 %copy-start.47 = (f32[1024]{0:T(1024)S(1)}, f32[1024]{0:T(1024)}, u32[]{:S(2)}) copy-start(f32[1024]{0:T(1024)} %copy-done.46) | copy-start | bytes 12292
  567.7 251.8 %copy-start.49 = (f32[1024]{0:T(1024)S(1)}, f32[1024]{0:T(1024)}, u32[]{:S(2)}) copy-start(f32[1024]{0:T(1024)} %copy-done.48) | copy-start | bytes 12292
  567.7 251.8 %copy-start.55 = (f32[256]{0:T(256)S(1)}, f32[256]{0:T(256)}, u32[]{:S(2)}) copy-start(f32[256]{0:T(256)} %copy-done.54) | copy-start | bytes 3076
  567.7 254.1 %copy-start.61 = (f32[256]{0:T(256)S(1)}, f32[256]{0:T(256)}, u32[]{:S(2)}) copy-start(f32[256]{0:T(256)} %copy-done.60) | copy-start | bytes 3076
  567.7 254.1 %copy-start.59 = (f32[256]{0:T(256)S(1)}, f32[256]{0:T(256)}, u32[]{:S(2)}) copy-start(f32[256]{0:T(256)} %copy-done.58) | copy-start | bytes 3076
  819.5 243.2 %copy-start.3 = (f32[256,2048]{1,0:T(8,128)S(1)}, f32[256,2048]{1,0:T(8,128)}, u32[]{:S(2)}) copy-start(f32[256,2048]{1,0:T(8,128)} %reduce-scatter.9.cloned.1.call-done) | copy-start | bytes 6291460
  1066.9 175.2 %all-reduce.16.cloned.1.call-start = ((), (), s32[]{:S(2)}) async-start(), calls=%async_computation.11 | async-start | bytes 12582912 | tf_op jit(solution)/shard_map/psum | solution.py:391
  (87 other events, 506.3 us)
Sparse Core Ops, SparseCore 0:
  10.2 76.0 all-gather.7
  89.0 71.6 all-gather.3
  163.4 71.6 all-gather.5
  539.1 280.3 reduce-scatter.8
  823.4 86.9 reduce-scatter.6
  913.9 148.7 reduce-scatter.4
  1067.0 52.4 reduce-scatter.10
  1122.9 119.1 all-reduce.15
where the time goes:
time: 1270 us; the launch traced here: 1260 us
  waiting for transfers between devices  783 us (62%)
  matrix products  181 us (14%)
  local copies, waits for them, and re-layouts  143 us (11%)
  other arithmetic  115 us (9%)
  between operations  15.5 us (1%)
  loops' own time  12.9 us (1%)
    reduce_scatter x1, waiting for transfers between devices, on_device(): lax.psum_scatter(jnp.concatenate([jnp.einsum('tc,dc->td', qkv_grad, qkv_w...  248 us
    reduce_scatter x1, waiting for transfers between devices, on_device(): lax.psum_scatter(jnp.dot(merged, dense_weight, preferred_element_type=jnp...  152 us
    psum x1, waiting for transfers between devices, on_device(): lax.psum((qkv_weight_grad, qkv_bias_grad, dense_weight_grad, up_weight_gr...  116 us
    reduce_scatter x1, waiting for transfers between devices, on_device(): lax.psum_scatter(jnp.dot(activated, down_weight, preferred_element_type=j...  85.9 us
    all_gather x1, waiting for transfers between devices, on_device(): lax.all_gather(norm_values[0].astype(jnp.bfloat16), 'tensor', axis=0, til...  68.9 us
    all_gather x1, waiting for transfers between devices, on_device(): grad_whole = lax.all_gather(out_grad, 'tensor', axis=0, tiled=True)  64.1 us
    dynamic_update_slice x40, local copies, waits for them, and re-layouts, attend_forward(): lax.scan(advance, initial, (query_blocks, key_blocks, value_blocks, doc_b...  62.8 us
    reduce_scatter x1, waiting for transfers between devices, on_device(): lax.psum_scatter(jnp.stack([first_gain_grad, first_shift_grad, second_gai...  47 us
  transfers between devices with their start and end apart: 8, of which 7 were waited for; matrix products, arithmetic and copies ran while one was open for 31% of the time, Pallas kernels for 0%

commit v1 on v0

--- a/solution.py
+++ b/solution.py
@@ -309,7 +309,14 @@
         jnp.float32
     )
     layer_out = (local_rows + branch_total + out_bias.astype(jnp.float32)).astype(jnp.bfloat16)
-    grad_whole = lax.all_gather(out_grad, "tensor", axis=0, tiled=True)
+    devices = lax.axis_size("tensor")
+    route = [(i, (i + 1) % devices) for i in range(devices)]
+    parts = [out_grad]
+    for far in range(1, devices):
+        parts = [lax.ppermute(parts[0], "tensor", route), *parts]
+    whole = jnp.concatenate(parts, axis=0)
+    places_2 = (lax.axis_index("tensor") + 1) * parts[-1].shape[0]
+    grad_whole = jnp.roll(whole, places_2, axis=0)
     merged_grad = jnp.einsum(
         "td,ed->te", grad_whole, dense_weight, preferred_element_type=jnp.float32
     )

time: 1270 us -> 1330 us (1.047)
  matrix products: 181 us -> 204 us
  waiting for transfers between devices: 783 us -> 803 us
  local copies, waits for them, and re-layouts: 143 us -> 157 us
    ppermute x0 -> x7, waiting for transfers between devices: none -> 151 us  [on_device(): parts = [lax.ppermute(parts[0], 'tensor', route), *parts]]
    all_gather x1, waiting for transfers between devices: 68.9 us -> 0.02 us  [on_device(): lax.all_gather(norm_values[0].astype(jnp.bfloat16), 'tensor', axis=0, til...]
    all_gather x1 -> x0, waiting for transfers between devices: 64.1 us -> none  [on_device(): grad_whole = lax.all_gather(out_grad, 'tensor', axis=0, tiled=True)]
    unnamed x135 -> x160, local copies, waits for them, and re-layouts: 25.3 us -> 35.2 us
  transfers between devices with their start and end apart: 8 -> 14, of which waited for: 7 -> 12; matrix products, arithmetic and copies ran while one was open for 31% -> 32% of each run, Pallas kernels for 0% -> 0%
where the time goes in v1:
time: 1330 us; the launch traced here: 1320 us
  waiting for transfers between devices  803 us (60%)
  matrix products  204 us (15%)
  local copies, waits for them, and re-layouts  157 us (12%)
  other arithmetic  120 us (9%)
  between operations  15.4 us (1%)
    reduce_scatter x1, waiting for transfers between devices, on_device(): lax.psum_scatter(jnp.concatenate([jnp.einsum('tc,dc->td', qkv_grad, qkv_w...  251 us
    reduce_scatter x1, waiting for transfers between devices, on_device(): lax.psum_scatter(jnp.dot(merged, dense_weight, preferred_element_type=jnp...  152 us
    ppermute x7, waiting for transfers between devices, on_device(): parts = [lax.ppermute(parts[0], 'tensor', route), *parts]  151 us
    psum x1, waiting for transfers between devices, on_device(): lax.psum((qkv_weight_grad, qkv_bias_grad, dense_weight_grad, up_weight_gr...  116 us
    reduce_scatter x1, waiting for transfers between devices, on_device(): lax.psum_scatter(jnp.dot(activated, down_weight, preferred_element_type=j...  85.9 us
    dynamic_update_slice x40, local copies, waits for them, and re-layouts, attend_forward(): lax.scan(advance, initial, (query_blocks, key_blocks, value_blocks, doc_b...  62.7 us
    reduce_scatter x1, waiting for transfers between devices, on_device(): lax.psum_scatter(jnp.stack([first_gain_grad, first_shift_grad, second_gai...  47.1 us
    unnamed x160, local copies, waits for them, and re-layouts  35.2 us
  transfers between devices with their start and end apart: 14, of which 12 were waited for; matrix products, arithmetic and copies ran while one was open for 32% of the time, Pallas kernels for 0%

profile of v1, /device:TPU:0, one launch (start us, length us, event | category | flops | bytes accessed | tf_op | source)
XLA Modules:
  0.0 1322.5 jit_solution(1625585084735843579)
XLA Ops:
  15.1 3.0 collective-permute-start
  18.1 17.5 %collective-permute-done = bf16[256,1024]{1,0:T(8,128)(2,1)S(1)} collective-permute-done((bf16[256,1024]{1,0:T(8,128)(2,1)}, bf16[256,1024]{1,0:T(8,128)(2,1)S(1)}, u32[]{:S(2)}, u32[]{:S(2)}) %collective-permute-start) | collective-permute-done | bytes 524320 | tf_op jit(solution)/shard_map/ppermute | solution.py:316
  36.0 25.5 %collective-permute-done.1 = bf16[256,1024]{1,0:T(8,128)(2,1)S(1)} collective-permute-done((bf16[256,1024]{1,0:T(8,128)(2,1)S(1)}, bf16[256,1024]{1,0:T(8,128)(2,1)S(1)}, u32[]{:S(2)}, u32[]{:S(2)}) %collective-permute-start.1) | collective-permute-done | bytes 524320 | tf_op jit(solution)/shard_map/ppermute | solution.py:316
  62.2 26.8 %collective-permute-done.2 = bf16[256,1024]{1,0:T(8,128)(2,1)S(1)} collective-permute-done((bf16[256,1024]{1,0:T(8,128)(2,1)S(1)}, bf16[256,1024]{1,0:T(8,128)(2,1)S(1)}, u32[]{:S(2)}, u32[]{:S(2)}) %collective-permute-start.2) | collective-permute-done | bytes 524320 | tf_op jit(solution)/shard_map/ppermute | solution.py:316
  89.8 26.7 %collective-permute-done.3 = bf16[256,1024]{1,0:T(8,128)(2,1)S(1)} collective-permute-done((bf16[256,1024]{1,0:T(8,128)(2,1)S(1)}, bf16[256,1024]{1,0:T(8,128)(2,1)S(1)}, u32[]{:S(2)}, u32[]{:S(2)}) %collective-permute-start.3) | collective-permute-done | bytes 524320 | tf_op jit(solution)/shard_map/ppermute | solution.py:316
  117.3 16.4 %collective-permute-done.4 = bf16[256,1024]{1,0:T(8,128)(2,1)} collective-permute-done((bf16[256,1024]{1,0:T(8,128)(2,1)S(1)}, bf16[256,1024]{1,0:T(8,128)(2,1)}, u32[]{:S(2)}, u32[]{:S(2)}) %collective-permute-start.4) | collective-permute-done | bytes 524320 | tf_op jit(solution)/shard_map/ppermute | solution.py:316
  138.0 9.6 collective-permute-done.5
  148.0 29.0 %collective-permute-done.6 = bf16[256,1024]{1,0:T(8,128)(2,1)S(1)} collective-permute-done((bf16[256,1024]{1,0:T(8,128)(2,1)}, bf16[256,1024]{1,0:T(8,128)(2,1)S(1)}, u32[]{:S(2)}, u32[]{:S(2)}) %collective-permute-start.6) | collective-permute-done | bytes 524320 | tf_op jit(solution)/shard_map/ppermute | solution.py:316
  188.1 5.9 fusion.339
  207.8 47.1 %while.89 = (s32[]{:T(128)}, f32[1,64,64]{2,1,0:T(8,128)S(1)}, f32[1,64]{1,0:T(1,128)S(1)}, f32[4,1,512,64]{2,3,1,0:T(8,128)}, f32[4,1,512,1]{2,3,1,0:T(1,128)},...) while((s32[]{:T(128)}, f32[1,64,64]{2,1,0:T(8,128)S(1)}, ...), condition=%wide.region_9.10_spmd.clone, body=%wide.region_6.9_spmd.clone.sunk | while | flops 266197760 | bytes 3652069 | solution.py:117
  262.0 42.9 %while.88 = (s32[]{:T(128)}, f32[1,64,64]{2,1,0:T(8,128)S(1)}, f32[1,64]{1,0:T(1,128)S(1)}, f32[4,1,512,64]{2,3,1,0:T(8,128)}, f32[4,1,512,1]{2,3,1,0:T(1,128)S(...) while((s32[]{:T(128)}, f32[1,64,64]{2,1,0:T(8,128)S(1)}, ...), condition=%wide.region_5.6_spmd.clone, body=%wide.region_2.5_spmd.clone.sunk | while | flops 266197760 | bytes 3652325 | solution.py:117
  306.7 136.4 %while.91 = (s32[]{:T(128)}, f32[1,64,64]{2,1,0:T(8,128)}, f32[1,64]{1,0:T(1,128)}, f32[4,1,512,64]{2,0,3,1:T(4,128)}, f32[4,1,512,64]{2,0,3,1:T(4,128)}, /*inde...) while((s32[]{:T(128)}, f32[1,64,64]{2,1,0:T(8,128)}, ...), condition=%wide.region_19.20_spmd.clone, body=%wide.region_16.19_spmd.clone.sunk | while | flops 942595712 | bytes 10778062 | solution.py:197
  325.8 3.6 dynamic_update_slice.133
  329.4 3.6 dynamic_update_slice.132
  360.1 3.6 dynamic_update_slice.133
  363.7 3.6 dynamic_update_slice.132
  394.3 3.6 dynamic_update_slice.133
  398.0 3.6 dynamic_update_slice.132
  428.6 3.6 dynamic_update_slice.133
  432.2 3.6 dynamic_update_slice.132
  444.8 113.4 %while.90 = (s32[]{:T(128)}, f32[1,64,64]{2,1,0:T(8,128)}, f32[1,64]{1,0:T(1,128)}, f32[4,1,512,64]{2,0,3,1:T(4,128)}, f32[4,1,512,64]{2,0,3,1:T(4,128)}, /*inde...) while((s32[]{:T(128)}, f32[1,64,64]{2,1,0:T(8,128)}, ...), condition=%wide.region_15.16_spmd.clone, body=%wide.region_12.15_spmd.clone.sunk | while | flops 942595712 | bytes 11842542 | solution.py:197
  462.0 3.6 dynamic_update_slice.130
  465.7 3.6 dynamic_update_slice.129
  490.5 3.6 dynamic_update_slice.130
  494.2 3.6 dynamic_update_slice.129
  518.9 3.6 dynamic_update_slice.130
  522.6 3.6 dynamic_update_slice.129
  547.4 3.6 dynamic_update_slice.130
  551.1 3.6 dynamic_update_slice.129
  567.2 5.7 fusion.343
  572.9 13.9 %multiply_convert_fusion = (bf16[2048,512]{1,0:T(8,128)(2,1)}, f32[2048,512]{1,0:T(8,128)S(1)}, f32[2048,512]{1,0:T(8,128)S(1)}) fusion(f32[512]{0:T(512)S(1)} %copy-done.66, bf16[2048,1024]{1,0:T(8,128)(2,1)} %all-gather.5.cloned.1.call-done, bf16[1024,512]{1,0:T(8,128)(2,1)S(1)} %copy-done), kind=kOutput, calls=%fused_computation.271 | convolution fusion | flops 2216689664 | bytes 15730688 | tf_op jit(solution)/shard_map/dot_general | solution.py:257
  586.8 6.3 convert_reduce_fusion.2
  597.2 6.3 pad_maximum_fusion
  603.6 6.2 convolution_convert_fusion
  613.5 4.5 fusion.342
  618.7 5.9 fusion.345
  624.6 6.1 fusion.190
  630.7 3.7 fusion.346
  634.4 251.1 %reduce-scatter.9.cloned.1.call-done = f32[256,2048]{1,0:T(8,128)} async-done(((f32[2048,2048]{1,0:T(8,128)}), f32[256,2048]{1,0:T(8,128)}) %reduce-scatter.9.cloned.1.call-update) | async-done | bytes 2097168 | tf_op jit(solution)/shard_map/reduce_scatter | solution.py:368
  887.8 2.6 fusion.215
  890.5 85.9 %reduce-scatter.7.cloned.1.call-done = bf16[256,1024]{1,0:T(8,128)(2,1)} async-done(((bf16[2048,1024]{1,0:T(8,128)(2,1)}), bf16[256,1024]{1,0:T(8,128)(2,1)}) %reduce-scatter.7.cloned.1.call-update) | async-done | bytes 524304 | tf_op jit(solution)/shard_map/reduce_scatter | solution.py:303
  976.4 152.2 %reduce-scatter.5.cloned.1.call-done = f32[256,1024]{1,0:T(8,128)} async-done(((f32[2048,1024]{1,0:T(8,128)}), f32[256,1024]{1,0:T(8,128)}) %reduce-scatter.5.cloned.1.call-update) | async-done | bytes 1048592 | tf_op jit(solution)/shard_map/reduce_scatter | solution.py:298
  1128.7 3.5 convert_reduce_fusion.5
  1132.9 3.9 fusion.192
  1138.5 47.1 %reduce-scatter.11.cloned.1.call-done = f32[5,128]{1,0:T(8,128)} async-done(((f32[5,1024]{1,0:T(8,128)}), f32[5,128]{1,0:T(8,128)}) %reduce-scatter.11.cloned.1.call-update) | async-done | bytes 2576 | tf_op jit(solution)/shard_map/reduce_scatter | solution.py:384
  1185.6 6.4 all-reduce.12
  1192.5 115.6 %all-reduce.16.cloned.1.call-done = (f32[1024,384]{1,0:T(8,128)}, f32[128,1024]{1,0:T(8,128)}, f32[1024,512]{1,0:T(8,128)}, f32[512,1024]{1,0:T(8,128)}) async-done(((f32[1024,384]{1,0:T(8,128)}, f32[128,1024]{1,0:T(8,128)}, f32[1024,512]{1,0:T(8,128)}, f32[512,1024]{1,0:T(8,128)}), (f32[1024,384]{1,0:T(8,128)}, f32[128,1024]{1,0:T(8,128)}, f32[1024,512]{1,0:T(8,128)}, ...) | async-done | bytes 6291472 | tf_op jit(solution)/shard_map/psum | solution.py:398
  1308.1 2.8 copy.264
  (684 shorter events, 346.7 us)
Async XLA Ops:
  7.2 565.7 %copy-start = (bf16[1024,512]{1,0:T(8,128)(2,1)S(1)}, bf16[1024,512]{1,0:T(8,128)(2,1)}, u32[]{:S(2)}) copy-start(bf16[1024,512]{1,0:T(8,128)(2,1)} %param.27) | copy-start | bytes 3145732
  7.2 127.4 %copy-start.34 = (s32[1,2048]{1,0:T(1,128)S(1)}, s32[1,2048]{1,0:T(1,128)}, u32[]{:S(2)}) copy-start(s32[1,2048]{1,0:T(1,128)} %param.36) | copy-start | bytes 24580
  7.2 130.2 %copy-start.67 = (bf16[512]{0:T(512)(128)(2,1)S(1)}, bf16[512]{0:T(512)(128)(2,1)}, u32[]{:S(2)}) copy-start(bf16[512]{0:T(512)(128)(2,1)} %param.28) | copy-start | bytes 3076
  7.2 130.8 %copy-start.68 = (bf16[384]{0:T(512)(128)(2,1)S(1)}, bf16[384]{0:T(512)(128)(2,1)}, u32[]{:S(2)}) copy-start(bf16[384]{0:T(512)(128)(2,1)} %param.25) | copy-start | bytes 2308
  7.2 140.4 %copy-start.57 = (f32[64,64]{1,0:T(8,128)S(1)}, f32[64,64]{1,0:T(8,128)}, u32[]{:S(2)}) copy-start(f32[64,64]{1,0:T(8,128)} %param.35) | copy-start | bytes 49156
  7.2 180.9 %all-gather.3.cloned.1.call-start = ((), (), s32[]{:S(2)}) async-start(), calls=%async_computation.4 | async-start | bytes 4718592 | tf_op jit(solution)/shard_map/all_gather | solution.py:248
  9.9 170.6 %copy-start.58 = (f32[256]{0:T(256)}, f32[256]{0:T(256)S(1)}, u32[]{:S(2)}) copy-start(f32[256]{0:T(256)S(1)} %fusion.314) | copy-start | bytes 3076
  15.1 557.8 %all-gather.5.cloned.1.call-start = ((), (), s32[]{:S(2)}) async-start(), calls=%async_computation.6 | async-start | bytes 4718592 | tf_op jit(solution)/shard_map/all_gather | solution.py:249
  15.1 20.5 %collective-permute-start = (bf16[256,1024]{1,0:T(8,128)(2,1)}, bf16[256,1024]{1,0:T(8,128)(2,1)S(1)}, u32[]{:S(2)}, u32[]{:S(2)}) collective-permute-start(bf16[256,1024]{1,0:T(8,128)(2,1)} %param.37), channel_id=1, source_target_pairs={{0,1},{1,2},{2,3},{3,4},{4,5},{5,6},{6,7},{7,0},{8,9},{9,10},{10,1... | collective-permute-start | bytes 1572872 | tf_op jit(solution)/shard_map/ppermute | solution.py:316
  35.6 25.8 %collective-permute-start.1 = (bf16[256,1024]{1,0:T(8,128)(2,1)S(1)}, bf16[256,1024]{1,0:T(8,128)(2,1)S(1)}, u32[]{:S(2)}, u32[]{:S(2)}) collective-permute-start(bf16[256,1024]{1,0:T(8,128)(2,1)S(1)} %collective-permute-done), channel_id=1, source_target_pairs={{0,1},{1,2},{2,3},{3,4},{4,5},{5,6},{6,7},{7,0},{8,9},{9,10},{10,1... | collective-permute-start | bytes 1572872 | tf_op jit(solution)/shard_map/ppermute | solution.py:316
  62.2 26.8 %collective-permute-start.2 = (bf16[256,1024]{1,0:T(8,128)(2,1)S(1)}, bf16[256,1024]{1,0:T(8,128)(2,1)S(1)}, u32[]{:S(2)}, u32[]{:S(2)}) collective-permute-start(bf16[256,1024]{1,0:T(8,128)(2,1)S(1)} %collective-permute-done.1), channel_id=1, source_target_pairs={{0,1},{1,2},{2,3},{3,4},{4,5},{5,6},{6,7},{7,0},{8,9},{9,10},{10,1... | collective-permute-start | bytes 1572872 | tf_op jit(solution)/shard_map/ppermute | solution.py:316
  89.8 26.7 %collective-permute-start.3 = (bf16[256,1024]{1,0:T(8,128)(2,1)S(1)}, bf16[256,1024]{1,0:T(8,128)(2,1)S(1)}, u32[]{:S(2)}, u32[]{:S(2)}) collective-permute-start(bf16[256,1024]{1,0:T(8,128)(2,1)S(1)} %collective-permute-done.2), channel_id=1, source_target_pairs={{0,1},{1,2},{2,3},{3,4},{4,5},{5,6},{6,7},{7,0},{8,9},{9,10},{10,1... | collective-permute-start | bytes 1572872 | tf_op jit(solution)/shard_map/ppermute | solution.py:316
  117.3 16.4 %collective-permute-start.4 = (bf16[256,1024]{1,0:T(8,128)(2,1)S(1)}, bf16[256,1024]{1,0:T(8,128)(2,1)}, u32[]{:S(2)}, u32[]{:S(2)}) collective-permute-start(bf16[256,1024]{1,0:T(8,128)(2,1)S(1)} %collective-permute-done.3), channel_id=1, source_target_pairs={{0,1},{1,2},{2,3},{3,4},{4,5},{5,6},{6,7},{7,0},{8,9},{9,10},{10,1... | collective-permute-start | bytes 1572872 | tf_op jit(solution)/shard_map/ppermute | solution.py:316
  133.6 13.9 %collective-permute-start.5 = (bf16[256,1024]{1,0:T(8,128)(2,1)}, bf16[256,1024]{1,0:T(8,128)(2,1)}, u32[]{:S(2)}, u32[]{:S(2)}) collective-permute-start(bf16[256,1024]{1,0:T(8,128)(2,1)} %collective-permute-done.4), channel_id=1, source_target_pairs={{0,1},{1,2},{2,3},{3,4},{4,5},{5,6},{6,7},{7,0},{8,9},{9,10},{10,1... | collective-permute-start | bytes 1572872 | tf_op jit(solution)/shard_map/ppermute | solution.py:316
  133.7 47.0 %copy-start.7 = (bf16[256,1024]{1,0:T(8,128)(2,1)S(1)}, bf16[256,1024]{1,0:T(8,128)(2,1)}, u32[]{:S(2)}) copy-start(bf16[256,1024]{1,0:T(8,128)(2,1)} %param.37) | copy-start | bytes 1572868
  133.7 751.8 %reduce-scatter.9.cloned.1.call-start = ((), (), s32[]{:S(2)}) async-start(), calls=%async_computation.8 | async-start | bytes 18874368 | tf_op jit(solution)/shard_map/reduce_scatter | solution.py:368
  133.8 46.8 %copy-start.17 = (bf16[4,1,512,64]{2,3,1,0:T(8,128)(2,1)}, bf16[4,1,512,64]{2,3,1,0:T(8,128)(2,1)S(1)}, u32[]{:S(2)}) copy-start(bf16[4,1,512,64]{2,3,1,0:T(8,128)(2,1)S(1)} %fusion.336) | copy-start | bytes 786436
  138.0 42.5 %copy-start.26 = (bf16[256,1024]{1,0:T(8,128)(2,1)S(1)}, bf16[256,1024]{1,0:T(8,128)(2,1)}, u32[]{:S(2)}) copy-start(bf16[256,1024]{1,0:T(8,128)(2,1)} %copy-done.25) | copy-start | bytes 1572868
  138.0 42.5 %copy-start.24 = (bf16[256,1024]{1,0:T(8,128)(2,1)S(1)}, bf16[256,1024]{1,0:T(8,128)(2,1)}, u32[]{:S(2)}) copy-start(bf16[256,1024]{1,0:T(8,128)(2,1)} %copy-done.23) | copy-start | bytes 1572868
  147.6 29.4 %collective-permute-start.6 = (bf16[256,1024]{1,0:T(8,128)(2,1)}, bf16[256,1024]{1,0:T(8,128)(2,1)S(1)}, u32[]{:S(2)}, u32[]{:S(2)}) collective-permute-start(bf16[256,1024]{1,0:T(8,128)(2,1)} %collective-permute-done.5), channel_id=1, source_target_pairs={{0,1},{1,2},{2,3},{3,4},{4,5},{5,6},{6,7},{7,0},{8,9},{9,10},{10,1... | collective-permute-start | bytes 1572872 | tf_op jit(solution)/shard_map/ppermute | solution.py:316
  147.6 51.0 %copy-start.62 = (f32[8]{0:T(128)}, f32[8]{0:T(128)S(1)}, u32[]{:S(2)}) copy-start(f32[8]{0:T(128)S(1)} %negate_power_fusion) | copy-start | bytes 100
  147.6 50.9 %copy-start.52 = (f32[2048]{0:T(1024)}, f32[2048]{0:T(1024)S(1)}, u32[]{:S(2)}) copy-start(f32[2048]{0:T(1024)S(1)} %fusion.310) | copy-start | bytes 24580
  148.0 109.7 %copy-start.15 = (f32[64,64]{1,0:T(8,128)}, f32[64,64]{1,0:T(8,128)S(1)}, u32[]{:S(2)}) copy-start(f32[64,64]{1,0:T(8,128)S(1)} %fusion.301) | copy-start | bytes 49156
  207.8 47.1 %copy-start.38 = (f32[2048,8]{0,1:T(8,128)S(1)}, f32[2048,8]{0,1:T(8,128)}, u32[]{:S(2)}) copy-start(f32[2048,8]{0,1:T(8,128)} %get-tuple-element.1292) | copy-start | bytes 196612
  207.8 47.1 %copy-start.39 = (f32[2048,8]{0,1:T(8,128)S(1)}, f32[2048,8]{0,1:T(8,128)}, u32[]{:S(2)}) copy-start(f32[2048,8]{0,1:T(8,128)} %get-tuple-element.1293) | copy-start | bytes 196612
  316.4 16.6 %copy-start.43 = (s32[1,1,512]{2,1,0:T(1,128)S(1)}, s32[1,1,512]{2,1,0:T(1,128)}, u32[]{:S(2)}) copy-start(s32[1,1,512]{2,1,0:T(1,128)} %copy-done.42) | copy-start | bytes 6148 | tf_op jit(solution)/shard_map/while
  350.1 17.3 %copy-start.43 = (s32[1,1,512]{2,1,0:T(1,128)S(1)}, s32[1,1,512]{2,1,0:T(1,128)}, u32[]{:S(2)}) copy-start(s32[1,1,512]{2,1,0:T(1,128)} %copy-done.42) | copy-start | bytes 6148 | tf_op jit(solution)/shard_map/while
  357.7 14.6 %copy-start.40 = (f32[512]{0:T(512)S(1)}, f32[512]{0:T(512)}, u32[]{:S(2)}) copy-start(f32[512]{0:T(512)} %get-tuple-element.1745) | copy-start | bytes 6148 | tf_op jit(solution)/shard_map/while
  384.3 17.3 %copy-start.43 = (s32[1,1,512]{2,1,0:T(1,128)S(1)}, s32[1,1,512]{2,1,0:T(1,128)}, u32[]{:S(2)}) copy-start(s32[1,1,512]{2,1,0:T(1,128)} %copy-done.42) | copy-start | bytes 6148 | tf_op jit(solution)/shard_map/while
  418.6 17.3 %copy-start.43 = (s32[1,1,512]{2,1,0:T(1,128)S(1)}, s32[1,1,512]{2,1,0:T(1,128)}, u32[]{:S(2)}) copy-start(s32[1,1,512]{2,1,0:T(1,128)} %copy-done.42) | copy-start | bytes 6148 | tf_op jit(solution)/shard_map/while
  445.0 16.1 %copy-start.3 = (bf16[4,1,512,64]{3,2,1,0:T(8,128)(2,1)S(1)}, bf16[4,1,512,64]{3,2,1,0:T(8,128)(2,1)}, u32[]{:S(2)}) copy-start(bf16[4,1,512,64]{3,2,1,0:T(8,128)(2,1)} %get-tuple-element.1948) | copy-start | bytes 786436 | tf_op jit(solution)/shard_map/while
  472.8 16.8 %copy-start.3 = (bf16[4,1,512,64]{3,2,1,0:T(8,128)(2,1)S(1)}, bf16[4,1,512,64]{3,2,1,0:T(8,128)(2,1)}, u32[]{:S(2)}) copy-start(bf16[4,1,512,64]{3,2,1,0:T(8,128)(2,1)} %get-tuple-element.1948) | copy-start | bytes 786436 | tf_op jit(solution)/shard_map/while
  482.6 15.2 %copy-start.45 = (s32[1,1,512]{2,1,0:T(1,128)S(1)}, s32[1,1,512]{2,1,0:T(1,128)}, u32[]{:S(2)}) copy-start(s32[1,1,512]{2,1,0:T(1,128)} %copy-done.44) | copy-start | bytes 6148 | tf_op jit(solution)/shard_map/while
  501.3 16.7 %copy-start.3 = (bf16[4,1,512,64]{3,2,1,0:T(8,128)(2,1)S(1)}, bf16[4,1,512,64]{3,2,1,0:T(8,128)(2,1)}, u32[]{:S(2)}) copy-start(bf16[4,1,512,64]{3,2,1,0:T(8,128)(2,1)} %get-tuple-element.1948) | copy-start | bytes 786436 | tf_op jit(solution)/shard_map/while
  511.0 15.2 %copy-start.45 = (s32[1,1,512]{2,1,0:T(1,128)S(1)}, s32[1,1,512]{2,1,0:T(1,128)}, u32[]{:S(2)}) copy-start(s32[1,1,512]{2,1,0:T(1,128)} %copy-done.44) | copy-start | bytes 6148 | tf_op jit(solution)/shard_map/while
  529.7 16.8 %copy-start.3 = (bf16[4,1,512,64]{3,2,1,0:T(8,128)(2,1)S(1)}, bf16[4,1,512,64]{3,2,1,0:T(8,128)(2,1)}, u32[]{:S(2)}) copy-start(bf16[4,1,512,64]{3,2,1,0:T(8,128)(2,1)} %get-tuple-element.1948) | copy-start | bytes 786436 | tf_op jit(solution)/shard_map/while
  539.5 15.2 %copy-start.45 = (s32[1,1,512]{2,1,0:T(1,128)S(1)}, s32[1,1,512]{2,1,0:T(1,128)}, u32[]{:S(2)}) copy-start(s32[1,1,512]{2,1,0:T(1,128)} %copy-done.44) | copy-start | bytes 6148 | tf_op jit(solution)/shard_map/while
  567.1 51.6 %copy-start.4 = (bf16[2048,384]{0,1:T(8,128)(2,1)}, bf16[2048,384]{0,1:T(8,128)(2,1)S(1)}, u32[]{:S(2)}) copy-start(bf16[2048,384]{0,1:T(8,128)(2,1)S(1)} %constant_dynamic-update-slice_fusion.22) | copy-start | bytes 4718596
  603.5 372.9 %reduce-scatter.7.cloned.1.call-start = ((), (), s32[]{:S(2)}) async-start(), calls=%async_computation.7 | async-start | bytes 4718592 | tf_op jit(solution)/shard_map/reduce_scatter | solution.py:303
  609.8 518.8 %reduce-scatter.5.cloned.1.call-start = ((), (), s32[]{:S(2)}) async-start(), calls=%async_computation.5 | async-start | bytes 9437184 | tf_op jit(solution)/shard_map/reduce_scatter | solution.py:298
  618.1 567.5 %reduce-scatter.11.cloned.1.call-start = ((), (), s32[]{:S(2)}) async-start(), calls=%async_computation.9 | async-start | bytes 36864 | tf_op jit(solution)/shard_map/reduce_scatter | solution.py:384
  630.7 254.8 %copy-start.49 = (f32[1024]{0:T(1024)S(1)}, f32[1024]{0:T(1024)}, u32[]{:S(2)}) copy-start(f32[1024]{0:T(1024)} %copy-done.48) | copy-start | bytes 12292
  630.7 254.8 %copy-start.51 = (f32[1024]{0:T(1024)S(1)}, f32[1024]{0:T(1024)}, u32[]{:S(2)}) copy-start(f32[1024]{0:T(1024)} %copy-done.50) | copy-start | bytes 12292
  630.7 254.8 %copy-start.56 = (f32[256]{0:T(256)S(1)}, f32[256]{0:T(256)}, u32[]{:S(2)}) copy-start(f32[256]{0:T(256)} %copy-done.55) | copy-start | bytes 3076
  630.7 257.1 %copy-start.61 = (f32[256]{0:T(256)S(1)}, f32[256]{0:T(256)}, u32[]{:S(2)}) copy-start(f32[256]{0:T(256)} %copy-done.60) | copy-start | bytes 3076
  630.7 257.1 %copy-start.59 = (f32[256]{0:T(256)S(1)}, f32[256]{0:T(256)}, u32[]{:S(2)}) copy-start(f32[256]{0:T(256)} %copy-done.58) | copy-start | bytes 3076
  885.5 243.1 %copy-start.2 = (f32[256,2048]{1,0:T(8,128)S(1)}, f32[256,2048]{1,0:T(8,128)}, u32[]{:S(2)}) copy-start(f32[256,2048]{1,0:T(8,128)} %reduce-scatter.9.cloned.1.call-done) | copy-start | bytes 6291460
  1132.9 175.2 %all-reduce.16.cloned.1.call-start = ((), (), s32[]{:S(2)}) async-start(), calls=%async_computation.10 | async-start | bytes 12582912 | tf_op jit(solution)/shard_map/psum | solution.py:398
  (70 other events, 386.9 us)
Sparse Core Ops, SparseCore 0:
  15.2 104.7 all-gather.2
  133.8 85.8 all-gather.4
  603.7 281.7 reduce-scatter.8
  889.4 86.9 reduce-scatter.6
  979.9 148.7 reduce-scatter.4
  1133.0 52.5 reduce-scatter.10
  1188.9 119.1 all-reduce.15
